TPU v7x, 32 devices: a whole 2x2x4 slice. The times are simulated.
32 devices in a mesh: wide: 8 (over z, y), narrow: 4 (over x, core).
Axes of the slice: x: 2, y: 2, z: 4, core: 2. Of those that a mesh axis runs over, the one named last changes fastest.
Arguments:
- residual: float32 [8, 4, 6, 192, 512], P('wide', 'narrow'), may hold values from -6 to 6
- face_schur: float32 [8, 4, 6, 192, 192], P('wide', 'narrow'), may hold values from -0.5 to 1.5, as said below
- local_solver: bfloat16 [8, 4, 1152, 1152], P('wide', 'narrow'), may hold values from -0.1875 to 0.1875
- interface_functional_set: float32 [3, 192, 16], replicated, may hold values from -0.4375 to 0.4375
- coarse_inverse: float32 [1536, 1536], P('wide', 'narrow'), may hold values from -0.3125 to 0.3125
Outputs:
- preconditioned: float32 [8, 4, 3, 192, 512], P('wide', 'narrow')
Inputs may be any that keep to these rules, and one draw needn't show every extreme that they name: `face_schur`: every face block is symmetric positive definite.
All inputs are finite; a program needn't handle non-finite values. Where the computation divides by a largest or mean magnitude, that divisor is 1e-20 or more.
Results may differ from a plain program's by a relative error of at most 0.002.
Values sent between devices are 32-bit elements; how exact they have to be, the bound alone decides.
No kernel may reach another device: no remote copies, remote signals or barrier semaphores. Data moves between devices by JAX's collectives and lax.ppermute only.
A program may use at most 64 MiB of HBM per device.

v0:
```python
import jax
import jax.numpy as jnp
from jax import lax
from jax.sharding import PartitionSpec as P

NS_STEPS = 12
exact_arithmetic_mode = lax.Precision.HIGHEST


def passed_along(value, axis, steps):
    count = lax.axis_size(axis)
    pairs = [(source, (source + steps) % count) for source in range(count)]
    return lax.ppermute(value, axis, pairs)


def newton_schulz(matrices):
    row_sums = jnp.max(jnp.sum(jnp.abs(matrices), axis=2), axis=1)
    approx = matrices / (row_sums * row_sums)[:, None, None]
    for iteration in range(NS_STEPS):
        product = jnp.einsum("bij,bjk->bik", matrices, approx, precision=exact_arithmetic_mode)
        approx = 2.0 * approx - jnp.einsum(
            "bij,bjk->bik", approx, product, precision=exact_arithmetic_mode
        )
    return approx


def apply_faces(blocks, fields):
    return jnp.einsum("fij,fjr->fir", blocks, fields, precision=exact_arithmetic_mode)


def per_device(residual, face_schur, local_solver, interface_functional_set, coarse_inverse):
    blocks = face_schur[0, 0]
    face_loads = residual[0, 0]
    face_order = blocks.shape[1]
    columns_count = face_loads.shape[2]
    wide_low = jnp.concatenate([blocks[0], face_loads[0]], axis=1)
    wide_above = passed_along(wide_low, "wide", -1)
    narrow_low = jnp.concatenate([blocks[2], face_loads[2]], axis=1)
    narrow_above = passed_along(narrow_low, "narrow", -1)
    owned_sums = jnp.stack(
        [
            blocks[1] + wide_above[:, :face_order],
            blocks[3] + narrow_above[:, :face_order],
            blocks[4] + blocks[5],
        ],
        axis=0,
    )
    owned_values = jnp.stack(
        [
            face_loads[1] + wide_above[:, face_order:],
            face_loads[3] + narrow_above[:, face_order:],
            face_loads[4] + face_loads[5],
        ],
        axis=0,
    )
    owned_inverse = newton_schulz(owned_sums)
    owned_scaled = apply_faces(owned_inverse, owned_values)
    wide_below = passed_along(owned_scaled[0], "wide", 1)
    narrow_below = passed_along(owned_scaled[1], "narrow", 1)
    face_scaled = jnp.stack(
        [
            wide_below,
            owned_scaled[0],
            narrow_below,
            owned_scaled[1],
            owned_scaled[2],
            owned_scaled[2],
        ],
        axis=0,
    )
    restricted_residual = jnp.einsum(
        "psk,pse->pke", interface_functional_set, owned_values, precision=exact_arithmetic_mode
    )
    restricted_residual = restricted_residual.reshape(-1, columns_count)
    incomplete_total = jnp.dot(
        coarse_inverse,
        lax.all_gather(restricted_residual, "wide", axis=0, tiled=True),
        precision=exact_arithmetic_mode,
        preferred_element_type=jnp.float32,
    )
    own_rows = restricted_residual.shape[0]
    summed = lax.psum(incomplete_total, "narrow")
    own_coarse = lax.dynamic_slice_in_dim(summed, lax.axis_index("narrow") * own_rows, own_rows, 0)
    local_loads = apply_faces(blocks, face_scaled).astype(jnp.bfloat16)
    flattened = local_loads.reshape(-1, columns_count)
    solved = jnp.dot(local_solver[0, 0], flattened, preferred_element_type=jnp.float32)
    solved = solved.reshape(6, face_order, columns_count)
    weighted = apply_faces(blocks, solved)
    wide_back = passed_along(weighted[0], "wide", -1)
    narrow_back = passed_along(weighted[2], "narrow", -1)
    combined = jnp.stack(
        [weighted[1] + wide_back, weighted[3] + narrow_back, weighted[4] + weighted[5]], axis=0
    )
    local_part = apply_faces(owned_inverse, combined)
    update_increment = own_coarse.reshape(3, -1, columns_count)
    coarse_component = jnp.einsum(
        "fek,fkg->feg", interface_functional_set, update_increment, precision=exact_arithmetic_mode
    )
    output_answer = local_part + coarse_component
    return output_answer[None, None]


def solution(mesh):
    placed = (
        P("wide", "narrow", None, None, None),
        P("wide", "narrow", None, None, None),
        P("wide", "narrow", None, None),
        P(),
        P("wide", "narrow"),
    )
    return jax.shard_map(
        per_device,
        mesh=mesh,
        in_specs=placed,
        out_specs=P("wide", "narrow", None, None, None),
        check_vma=False,
    )
```

profile of v0, /device:TPU:0, one launch (start us, length us, event | category | flops | bytes accessed | tf_op | source)
XLA Modules:
  0.0 147.2 jit_solution(12711466252790806071)
XLA Ops:
  6.5 1.4 add_bitcast_fusion.1
  8.0 2.3 %slice_bitcast_fusion.6 = (f32[192,512]{1,0:T(8,128)S(1)}, f32[192,512]{1,0:T(8,128)S(1)}, f32[1,192,512]{2,1,0:T(8,128)}) fusion(f32[1,1,6,192,512]{4,3,2,1,0:T(8,128)} %param.5), kind=kLoop, calls=%fused_computation.57 | loop fusion | flops 98304 | bytes 2752512 | tf_op jit(solution)/shard_map/squeeze | solution.py:36
  10.4 2.5 %collective-permute-start.1 = (f32[192,704]{1,0:T(8,128)S(1)}, f32[192,704]{1,0:T(8,128)S(1)}, u32[]{:S(2)}, u32[]{:S(2)}) collective-permute-start(f32[192,704]{1,0:T(8,128)S(1)} %pad_maximum_fusion.4), channel_id=1, source_target_pairs={{0,3},{1,0},{2,1},{3,2},{4,7},{5,4},{6,5},{7,6},{8,11},{9,8},{10,9... | collective-permute-start | bytes 1622024 | tf_op jit(solution)/shard_map/ppermute | solution.py:13
  13.1 4.6 %collective-permute-start = (f32[192,704]{1,0:T(8,128)S(1)}, f32[192,704]{1,0:T(8,128)S(1)}, u32[]{:S(2)}, u32[]{:S(2)}) collective-permute-start(f32[192,704]{1,0:T(8,128)S(1)} %pad_maximum_fusion.3), channel_id=1, source_target_pairs={{0,28},{4,0},{8,4},{12,8},{16,12},{20,16},{24,20},{28,24},{1,29},{... | collective-permute-start | bytes 1622024 | tf_op jit(solution)/shard_map/ppermute | solution.py:13
  17.7 2.6 %collective-permute-done.1 = f32[192,704]{1,0:T(8,128)S(1)} collective-permute-done((f32[192,704]{1,0:T(8,128)S(1)}, f32[192,704]{1,0:T(8,128)S(1)}, u32[]{:S(2)}, u32[]{:S(2)}) %collective-permute-start.1) | collective-permute-done | bytes 540704 | tf_op jit(solution)/shard_map/ppermute | solution.py:13
  20.3 9.7 %collective-permute-done = f32[192,704]{1,0:T(8,128)S(1)} collective-permute-done((f32[192,704]{1,0:T(8,128)S(1)}, f32[192,704]{1,0:T(8,128)S(1)}, u32[]{:S(2)}, u32[]{:S(2)}) %collective-permute-start) | collective-permute-done | bytes 540704 | tf_op jit(solution)/shard_map/ppermute | solution.py:13
  30.0 1.3 fusion.23
  31.6 0.8 fusion.11
  32.4 0.8 convolution_subtract_fusion.11
  33.2 0.7 fusion.37
  33.9 0.7 convolution_subtract_fusion.10
  34.7 0.7 fusion.36
  35.4 0.7 convolution_subtract_fusion.9
  36.1 0.7 fusion.35
  36.8 0.7 convolution_subtract_fusion.8
  37.6 0.7 fusion.34
  38.3 0.7 convolution_subtract_fusion.7
  39.0 0.7 fusion.33
  39.7 0.7 convolution_subtract_fusion.6
  40.5 0.7 fusion.32
  41.2 0.7 convolution_subtract_fusion.5
  41.9 0.7 fusion.31
  43.4 0.9 fusion.30
  45.0 0.7 fusion.29
  46.4 0.7 fusion.28
  47.9 0.7 fusion.27
  49.9 1.4 fusion.19
  51.3 1.2 fusion.10
  52.9 0.7 fusion.9
  53.6 12.1 %collective-permute-done.2 = f32[192,512]{1,0:T(8,128)S(1)} collective-permute-done((f32[192,512]{1,0:T(8,128)S(1)}, f32[192,512]{1,0:T(8,128)S(1)}, u32[]{:S(2)}, u32[]{:S(2)}) %collective-permute-start.2) | collective-permute-done | bytes 393248 | tf_op jit(solution)/shard_map/ppermute | solution.py:13
  65.8 0.8 slice_bitcast_fusion.4
  66.6 1.4 copy-done.4
  68.0 32.6 %all_gather.3 = f32[384,512]{1,0:T(8,128)S(1)} all-gather(f32[48,512]{1,0:T(8,128)S(1)} %bitcast.129), channel_id=1, replica_groups=mesh['wide'=8,'narrow'=4] {'wide'}, dimensions={0}, use_global_device_ids=true | all-gather | bytes 884736 | tf_op jit(solution)/shard_map/all_gather | solution.py:77
  100.6 1.6 %convolution_bitcast_fusion.3 = f32[192,512]{1,0:T(8,128)} fusion(f32[384,512]{1,0:T(8,128)S(1)} %all_gather.3, f32[192,384]{1,0:T(8,128)S(1)} %copy-done.11), kind=kOutput, calls=%fused_computation.19 | convolution fusion | flops 452984832 | bytes 1474560 | tf_op jit(solution)/shard_map/dot_general | solution.py:75
  102.3 1.8 %bitcast_dynamic-update-slice_fusion = f32[6,192,512]{2,1,0:T(8,128)} fusion(f32[6,192,512]{2,1,0:T(8,128)} %copy-done.4, f32[192,512]{1,0:T(8,128)} %collective-permute-done.3), kind=kLoop, calls=%fused_computation.53 | loop fusion | bytes 786432
  104.1 2.2 %slice_dynamic-update-slice_fusion = f32[6,192,512]{2,1,0:T(8,128)} fusion(f32[6,192,512]{2,1,0:T(8,128)} %bitcast_dynamic-update-slice_fusion, f32[3,192,512]{2,1,0:T(8,128)} %copy-done.1), kind=kLoop, calls=%fused_computation.30 | loop fusion | bytes 1572864
  106.2 1.8 %slice_dynamic-update-slice_fusion.1 = f32[6,192,512]{2,1,0:T(8,128)} fusion(f32[6,192,512]{2,1,0:T(8,128)} %slice_dynamic-update-slice_fusion, f32[3,192,512]{2,1,0:T(8,128)} %copy-done.1), kind=kLoop, calls=%fused_computation.47 | loop fusion | bytes 786432 | tf_op jit(solution)/shard_map/stack | solution.py:60
  108.0 4.0 %convolution_convert_fusion = bf16[6,512,192]{1,2,0:T(8,128)(2,1)S(1)} fusion(f32[6,192,512]{2,1,0:T(8,128)} %slice_dynamic-update-slice_fusion.1, f32[1,1,6,192,192]{4,3,2,1,0:T(8,128)S(1)} %copy-done.2), kind=kOutput, calls=%fused_computation.3 | convolution fusion | flops 1359544320 | bytes 4423680 | tf_op jit(solution)/shard_map/fij,fjr->fir/dot_general | solution.py:28
  112.0 3.4 %convolution_bitcast_fusion = f32[1152,512]{0,1:T(8,128)} fusion(bf16[1152,512]{1,0:T(8,128)(2,1)S(1)} %bitcast.127, bf16[1,1,1152,1152]{3,2,1,0:T(8,128)(2,1)S(1)} %copy-done), kind=kOutput, calls=%fused_computation | convolution fusion | flops 1358954496 | bytes 6193152 | tf_op jit(solution)/shard_map/dot_general | solution.py:86
  115.4 3.1 %copy.8 = f32[1152,512]{1,0:T(8,128)} copy(f32[1152,512]{0,1:T(8,128)} %convolution_bitcast_fusion) | data formatting | bytes 4718592 | tf_op jit(solution)/shard_map/dot_general | solution.py:86
  118.5 4.3 %convolution_bitcast_fusion.1 = f32[6,192,512]{2,1,0:T(8,128)S(1)} fusion(f32[6,192,512]{2,1,0:T(8,128)} %bitcast.126, f32[1,1,6,192,192]{4,3,2,1,0:T(8,128)} %param.6), kind=kOutput, calls=%fused_computation.2 | convolution fusion | flops 1358954496 | bytes 5603328 | tf_op jit(solution)/shard_map/fij,fjr->fir/dot_general | solution.py:28
  122.8 1.1 slice_bitcast_fusion.2
  124.6 1.4 collective-permute-start.4
  126.0 8.5 %all-reduce.2.cloned.1.call-done = f32[192,512]{1,0:T(8,128)} async-done(((f32[192,512]{1,0:T(8,128)}), f32[192,512]{1,0:T(8,128)}) %all-reduce.2.cloned.1.call-update) | async-done | bytes 393232 | tf_op jit(solution)/shard_map/psum | solution.py:82
  134.5 0.9 constant_dynamic-slice_fusion
  135.4 1.1 convolution_bitcast_fusion.2
  136.6 1.5 %fusion.17 = (f32[1,192,512]{2,1,0:T(8,128)S(1)}, f32[1,192,512]{2,1,0:T(8,128)S(1)}) fusion(f32[192,512]{1,0:T(8,128)} %collective-permute-done.4, f32[6,192,512]{2,1,0:T(8,128)} %copy-done.3, f32[192,512]{1,0:T(8,128)} %collective-permute-done.5), kind=kLoop, calls=%fused_computation.46 | loop fusion | flops 196608 | bytes 2359296 | tf_op jit(solution)/shard_map/stack | solution.py:91
  138.1 2.2 %fusion.1 = f32[1,1,3,192,512]{4,3,2,1,0:T(8,128)} fusion(f32[3,192,512]{2,1,0:T(8,128)S(1)} %convolution_bitcast_fusion.2, f32[3,192,192]{2,1,0:T(8,128)S(1)} %convolution_subtract_fusion, f32[1,192,512]{2,1,0:T(8,128)S(1)} %copy-done.6, f32[1,192,512]{2,1,0:T(8,128)S(1)} %get-tuple-element.6, f32[1,192,512]{2,1,0:T(8,128)S(1)} %get-tuple-element.5), kind=kOutput, calls=%fused_computation.6 | convolution fusion | flops 680361984 | bytes 3981312 | tf_op jit(solution)/shard_map/fij,fjr->fir/dot_general | solution.py:28
  (45 shorter events, 5.9 us)
Async XLA Ops:
  6.5 105.5 %copy-start = (bf16[1,1,1152,1152]{3,2,1,0:T(8,128)(2,1)S(1)}, bf16[1,1,1152,1152]{3,2,1,0:T(8,128)(2,1)}, u32[]{:S(2)}) copy-start(bf16[1,1,1152,1152]{3,2,1,0:T(8,128)(2,1)} %param.7) | copy-start | bytes 7962628
  6.5 128.0 %all-reduce.2.cloned.1.call-start = ((), (), s32[]{:S(2)}) async-start(), calls=%async_computation | async-start | bytes 786432 | tf_op jit(solution)/shard_map/psum | solution.py:82
  10.4 9.9 %collective-permute-start.1 = (f32[192,704]{1,0:T(8,128)S(1)}, f32[192,704]{1,0:T(8,128)S(1)}, u32[]{:S(2)}, u32[]{:S(2)}) collective-permute-start(f32[192,704]{1,0:T(8,128)S(1)} %pad_maximum_fusion.4), channel_id=1, source_target_pairs={{0,3},{1,0},{2,1},{3,2},{4,7},{5,4},{6,5},{7,6},{8,11},{9,8},{10,9... | collective-permute-start | bytes 1622024 | tf_op jit(solution)/shard_map/ppermute | solution.py:13
  13.1 16.9 %collective-permute-start = (f32[192,704]{1,0:T(8,128)S(1)}, f32[192,704]{1,0:T(8,128)S(1)}, u32[]{:S(2)}, u32[]{:S(2)}) collective-permute-start(f32[192,704]{1,0:T(8,128)S(1)} %pad_maximum_fusion.3), channel_id=1, source_target_pairs={{0,28},{4,0},{8,4},{12,8},{16,12},{20,16},{24,20},{28,24},{1,29},{... | collective-permute-start | bytes 1622024 | tf_op jit(solution)/shard_map/ppermute | solution.py:13
  20.3 9.7 %copy-start.7 = (f32[192,704]{1,0:T(8,128)}, f32[192,704]{1,0:T(8,128)S(1)}, u32[]{:S(2)}) copy-start(f32[192,704]{1,0:T(8,128)S(1)} %collective-permute-done.1) | copy-start | bytes 1622020
  30.0 1.3 copy-start.9
  48.6 1.1 copy-start.8
  48.6 1.2 copy-start.10
  49.9 1.4 copy-start.5
  51.3 1.6 %copy-start.12 = (f32[3,192,16]{1,2,0:T(8,128)S(1)}, f32[3,192,16]{1,2,0:T(8,128)}, u32[]{:S(2)}) copy-start(f32[3,192,16]{1,2,0:T(8,128)} %param.8) | copy-start | bytes 110596
  52.5 13.3 %copy-start.1 = (f32[3,192,512]{2,1,0:T(8,128)}, f32[3,192,512]{2,1,0:T(8,128)S(1)}, u32[]{:S(2)}) copy-start(f32[3,192,512]{2,1,0:T(8,128)S(1)} %fusion.10) | copy-start | bytes 3538948
  52.5 13.2 %collective-permute-start.2 = (f32[192,512]{1,0:T(8,128)S(1)}, f32[192,512]{1,0:T(8,128)S(1)}, u32[]{:S(2)}, u32[]{:S(2)}) collective-permute-start(f32[192,512]{1,0:T(8,128)S(1)} %slice_bitcast_fusion.7), channel_id=1, source_target_pairs={{0,4},{4,8},{8,12},{12,16},{16,20},{20,24},{24,28},{28,0},{1,5},{5... | collective-permute-start | bytes 1179656 | tf_op jit(solution)/shard_map/ppermute | solution.py:13
  65.8 34.8 %copy-start.11 = (f32[192,384]{1,0:T(8,128)S(1)}, f32[192,384]{1,0:T(8,128)}, u32[]{:S(2)}) copy-start(f32[192,384]{1,0:T(8,128)} %param.9) | copy-start | bytes 884740
  66.6 1.4 copy-start.4
  68.0 34.2 %collective-permute-start.3 = (f32[192,512]{1,0:T(8,128)}, f32[192,512]{1,0:T(8,128)}, u32[]{:S(2)}, u32[]{:S(2)}) collective-permute-start(f32[192,512]{1,0:T(8,128)} %get-tuple-element.15), channel_id=1, source_target_pairs={{0,1},{1,2},{2,3},{3,0},{4,5},{5,6},{6,7},{7,4},{8,9},{9,10},{10,1... | collective-permute-start | bytes 1179656 | tf_op jit(solution)/shard_map/ppermute | solution.py:13
  104.1 3.9 %copy-start.2 = (f32[1,1,6,192,192]{4,3,2,1,0:T(8,128)S(1)}, f32[1,1,6,192,192]{4,3,2,1,0:T(8,128)}, u32[]{:S(2)}) copy-start(f32[1,1,6,192,192]{4,3,2,1,0:T(8,128)} %param.6) | copy-start | bytes 2654212
  122.8 1.8 %copy-start.3 = (f32[6,192,512]{2,1,0:T(8,128)}, f32[6,192,512]{2,1,0:T(8,128)S(1)}, u32[]{:S(2)}) copy-start(f32[6,192,512]{2,1,0:T(8,128)S(1)} %convolution_bitcast_fusion.1) | copy-start | bytes 7077892
  124.6 11.9 %collective-permute-start.4 = (f32[192,512]{1,0:T(8,128)}, f32[192,512]{1,0:T(8,128)}, u32[]{:S(2)}, u32[]{:S(2)}) collective-permute-start(f32[192,512]{1,0:T(8,128)} %get-tuple-element.7), channel_id=1, source_target_pairs={{0,28},{4,0},{8,4},{12,8},{16,12},{20,16},{24,20},{28,24},{1,29},{... | collective-permute-start | bytes 1179656 | tf_op jit(solution)/shard_map/ppermute | solution.py:13
  126.0 10.6 %collective-permute-start.5 = (f32[192,512]{1,0:T(8,128)}, f32[192,512]{1,0:T(8,128)}, u32[]{:S(2)}, u32[]{:S(2)}) collective-permute-start(f32[192,512]{1,0:T(8,128)} %get-tuple-element.9), channel_id=1, source_target_pairs={{0,3},{1,0},{2,1},{3,2},{4,7},{5,4},{6,5},{7,6},{8,11},{9,8},{10,9... | collective-permute-start | bytes 1179656 | tf_op jit(solution)/shard_map/ppermute | solution.py:13
  136.5 1.6 %copy-start.6 = (f32[1,192,512]{2,1,0:T(8,128)S(1)}, f32[1,192,512]{2,1,0:T(8,128)}, u32[]{:S(2)}) copy-start(f32[1,192,512]{2,1,0:T(8,128)} %get-tuple-element.8) | copy-start | bytes 1179652
Sparse Core Ops, SparseCore 0:
  102.4 32.0 all-reduce.1
where the time goes:
time: 148 us; the launch traced here: 147 us
  matrix products  36.1 us (24%)
  waiting for transfers between devices  33 us (22%)
  blocking collectives  32.6 us (22%)
  between operations  13.8 us (9%)
  local copies, waits for them, and re-layouts  13.2 us (9%)
  other arithmetic  9.77 us (7%)
  starting transfers between devices  8.85 us (6%)
    all_gather x1, blocking collectives, per_device(): lax.all_gather(restricted_residual, 'wide', axis=0, tiled=True)  32.6 us
    ppermute x6, waiting for transfers between devices, passed_along(): return lax.ppermute(value, axis, pairs)  24.5 us
    dot_general x4, matrix products, apply_faces(): jnp.einsum('fij,fjr->fir', blocks, fields, precision=exact_arithmetic_mode)  11.7 us
    dot_general x12, matrix products, newton_schulz(): jnp.einsum('bij,bjk->bik', matrices, approx, precision=exact_arithmetic_m...  8.92 us
    ppermute x6, starting transfers between devices, passed_along(): return lax.ppermute(value, axis, pairs)  8.85 us
    dot_general x12, matrix products, newton_schulz(): jnp.einsum('bij,bjk->bik', approx, product, precision=exact_arithmetic_mode)  8.59 us
    psum x1, waiting for transfers between devices, per_device(): summed = lax.psum(incomplete_total, 'narrow')  8.51 us
    unnamed x29, local copies, waits for them, and re-layouts  6.61 us
  transfers between devices with their start and end apart: 7, of which 4 were waited for; matrix products, arithmetic and copies ran while one was open for 18% of the time, Pallas kernels for 0%

commit v1 on v0

--- a/solution.py
+++ b/solution.py
@@ -29,6 +29,21 @@
 
 
 def per_device(residual, face_schur, local_solver, interface_functional_set, coarse_inverse):
+
+    def part_panel_now(content, axis_tag="wide"):
+        newest = lax.axis_size(axis_tag)
+        met_up = lax.axis_index(axis_tag)
+        step_out, passed = (newest, met_up)
+        local_next, aux = (content, 1)
+        while aux < step_out:
+            frame_out = tuple(((u, u ^ aux) for u in range(step_out)))
+            long_array = lax.ppermute(local_next, axis_tag, perm=frame_out)
+            t1 = jnp.concatenate([local_next, long_array], axis=0)
+            mat_out = jnp.concatenate([long_array, local_next], axis=0)
+            local_next = jnp.where(passed & aux == 0, t1, mat_out)
+            aux = 2 * aux
+        return local_next
+
     blocks = face_schur[0, 0]
     face_loads = residual[0, 0]
     face_order = blocks.shape[1]
@@ -74,7 +89,7 @@
     restricted_residual = restricted_residual.reshape(-1, columns_count)
     incomplete_total = jnp.dot(
         coarse_inverse,
-        lax.all_gather(restricted_residual, "wide", axis=0, tiled=True),
+        part_panel_now(restricted_residual),
         precision=exact_arithmetic_mode,
         preferred_element_type=jnp.float32,
     )

time: 148 us -> 144 us (0.973)
  blocking collectives: 32.6 us -> 0 us
  starting transfers between devices: 8.85 us -> 26.1 us
  other arithmetic: 9.77 us -> 13.6 us
  waiting for transfers between devices: 33 us -> 36.8 us
  local copies, waits for them, and re-layouts: 13.2 us -> 16.2 us
    all_gather x1 -> x0, blocking collectives: 32.6 us -> none  [per_device(): lax.all_gather(restricted_residual, 'wide', axis=0, tiled=True)]
    ppermute x0 -> x3, waiting for transfers between devices: none -> 14.9 us  [part_panel_now(): long_array = lax.ppermute(local_next, axis_tag, perm=frame_out)]
    ppermute x6, starting transfers between devices: 8.85 us -> 23.3 us  [passed_along(): return lax.ppermute(value, axis, pairs)]
    ppermute x6, waiting for transfers between devices: 24.5 us -> 15.3 us  [passed_along(): return lax.ppermute(value, axis, pairs)]
    ppermute x0 -> x3, starting transfers between devices: none -> 2.75 us  [part_panel_now(): long_array = lax.ppermute(local_next, axis_tag, perm=frame_out)]
    unnamed x29 -> x23, local copies, waits for them, and re-layouts: 6.61 us -> 8.93 us
    psum x1, waiting for transfers between devices: 8.51 us -> 6.58 us  [per_device(): summed = lax.psum(incomplete_total, 'narrow')]
    select_n x0 -> x2, other arithmetic: none -> 1.85 us  [part_panel_now(): local_next = jnp.where(passed & aux == 0, t1, mat_out)]
  transfers between devices with their start and end apart: 7 -> 10, of which waited for: 4 -> 6; matrix products, arithmetic and copies ran while one was open for 18% -> 35% of each run, Pallas kernels for 0% -> 0%
where the time goes in v1:
time: 144 us
  matrix products  37.5 us (26%)
  waiting for transfers between devices  36.8 us (26%)
  starting transfers between devices  26.1 us (18%)
  local copies, waits for them, and re-layouts  16.2 us (11%)
  between operations  13.8 us (10%)
  other arithmetic  13.6 us (9%)
    ppermute x6, starting transfers between devices, passed_along(): return lax.ppermute(value, axis, pairs)  23.3 us
    ppermute x6, waiting for transfers between devices, passed_along(): return lax.ppermute(value, axis, pairs)  15.3 us
    ppermute x3, waiting for transfers between devices, part_panel_now(): long_array = lax.ppermute(local_next, axis_tag, perm=frame_out)  14.9 us
    dot_general x4, matrix products, apply_faces(): jnp.einsum('fij,fjr->fir', blocks, fields, precision=exact_arithmetic_mode)  11.7 us
    dot_general x12, matrix products, newton_schulz(): jnp.einsum('bij,bjk->bik', matrices, approx, precision=exact_arithmetic_m...  8.95 us
    unnamed x23, local copies, waits for them, and re-layouts  8.93 us
    dot_general x12, matrix products, newton_schulz(): jnp.einsum('bij,bjk->bik', approx, product, precision=exact_arithmetic_mode)  8.57 us
    psum x1, waiting for transfers between devices, per_device(): summed = lax.psum(incomplete_total, 'narrow')  6.58 us
  transfers between devices with their start and end apart: 10, of which 6 were waited for; matrix products, arithmetic and copies ran while one was open for 35% of the time, Pallas kernels for 0%

profile of v1, /device:TPU:0, one launch (start us, length us, event | category | flops | bytes accessed | tf_op | source)
XLA Modules:
  0.0 143.9 jit_solution(17679067203004192778)
XLA Ops:
  6.5 1.4 add_bitcast_fusion.1
  8.0 2.2 %slice_bitcast_fusion.6 = (f32[192,512]{1,0:T(8,128)S(1)}, f32[192,512]{1,0:T(8,128)S(1)}, f32[1,192,512]{2,1,0:T(8,128)}) fusion(f32[1,1,6,192,512]{4,3,2,1,0:T(8,128)} %param.5), kind=kLoop, calls=%fused_computation.64 | loop fusion | flops 98304 | bytes 2752512 | tf_op jit(solution)/shard_map/squeeze | solution.py:51
  10.2 1.0 pad_maximum_fusion.4
  11.2 2.4 %collective-permute-start.1 = (f32[192,704]{1,0:T(8,128)}, f32[192,704]{1,0:T(8,128)S(1)}, u32[]{:S(2)}, u32[]{:S(2)}) collective-permute-start(f32[192,704]{1,0:T(8,128)} %pad_maximum_fusion.4), channel_id=1, source_target_pairs={{0,3},{1,0},{2,1},{3,2},{4,7},{5,4},{6,5},{7,6},{8,11},{9,8},{10,9... | collective-permute-start | bytes 1622024 | tf_op jit(solution)/shard_map/ppermute | solution.py:13
  13.6 1.0 pad_maximum_fusion.3
  14.7 4.6 %collective-permute-start = (f32[192,704]{1,0:T(8,128)}, f32[192,704]{1,0:T(8,128)}, u32[]{:S(2)}, u32[]{:S(2)}) collective-permute-start(f32[192,704]{1,0:T(8,128)} %pad_maximum_fusion.3), channel_id=1, source_target_pairs={{0,28},{4,0},{8,4},{12,8},{16,12},{20,16},{24,20},{28,24},{1,29},{... | collective-permute-start | bytes 1622024 | tf_op jit(solution)/shard_map/ppermute | solution.py:13
  19.2 2.1 %collective-permute-done.1 = f32[192,704]{1,0:T(8,128)S(1)} collective-permute-done((f32[192,704]{1,0:T(8,128)}, f32[192,704]{1,0:T(8,128)S(1)}, u32[]{:S(2)}, u32[]{:S(2)}) %collective-permute-start.1) | collective-permute-done | bytes 540704 | tf_op jit(solution)/shard_map/ppermute | solution.py:13
  21.4 0.8 copy-done.8
  22.2 9.6 %collective-permute-done = f32[192,704]{1,0:T(8,128)} collective-permute-done((f32[192,704]{1,0:T(8,128)}, f32[192,704]{1,0:T(8,128)}, u32[]{:S(2)}, u32[]{:S(2)}) %collective-permute-start) | collective-permute-done | bytes 540704 | tf_op jit(solution)/shard_map/ppermute | solution.py:13
  31.9 1.3 fusion.29
  33.5 1.7 %fusion.24 = (f32[1,192,512]{2,1,0:T(8,128)S(1)}, f32[1,192,512]{2,1,0:T(8,128)S(1)}) fusion(f32[192,704]{1,0:T(8,128)} %collective-permute-done, f32[1,1,6,192,512]{4,3,2,1,0:T(8,128)} %param.5, f32[192,704]{1,0:T(8,128)} %copy-done.8), kind=kLoop, calls=%fused_computation.58 | loop fusion | flops 196608 | bytes 2359296 | tf_op jit(solution)/shard_map/stack | solution.py:63
  35.2 0.7 fusion.9
  36.3 0.8 fusion.16
  37.2 0.8 convolution_subtract_fusion.11
  37.9 0.7 fusion.44
  40.8 0.7 fusion.42
  42.3 0.7 fusion.41
  43.7 0.7 fusion.40
  46.6 0.9 fusion.38
  48.3 0.7 fusion.37
  54.1 1.2 fusion.10
  55.2 1.0 copy-done.1
  56.2 0.8 slice_bitcast_fusion.7
  57.0 1.7 %collective-permute-start.2 = (f32[192,512]{1,0:T(8,128)}, f32[192,512]{1,0:T(8,128)}, u32[]{:S(2)}, u32[]{:S(2)}) collective-permute-start(f32[192,512]{1,0:T(8,128)} %slice_bitcast_fusion.7), channel_id=1, source_target_pairs={{0,4},{4,8},{8,12},{12,16},{16,20},{20,24},{24,28},{28,0},{1,5},{5... | collective-permute-start | bytes 1179656 | tf_op jit(solution)/shard_map/ppermute | solution.py:13
  58.8 5.7 %collective-permute-done.7 = f32[96,512]{1,0:T(8,128)} collective-permute-done((f32[96,512]{1,0:T(8,128)S(1)}, f32[96,512]{1,0:T(8,128)}, u32[]{:S(2)}, u32[]{:S(2)}) %collective-permute-start.7) | collective-permute-done | bytes 196640 | tf_op jit(solution)/shard_map/ppermute | solution.py:40
  64.6 1.8 %maximum_select_fusion.2 = f32[192,512]{1,0:T(8,128)} fusion(f32[96,512]{1,0:T(8,128)} %collective-permute-done.7, f32[96,512]{1,0:T(8,128)S(1)} %maximum_select_fusion.3, pred[]{:T(512)S(6)} %eq.10), kind=kLoop, calls=%fused_computation.59 | loop fusion | flops 294912 | bytes 786433 | tf_op jit(solution)/shard_map/jit(_where)/select_n | solution.py:43
  66.4 2.3 %collective-permute-start.8 = (f32[192,512]{1,0:T(8,128)}, f32[192,512]{1,0:T(8,128)}, u32[]{:S(2)}, u32[]{:S(2)}) collective-permute-start(f32[192,512]{1,0:T(8,128)} %maximum_select_fusion.2), channel_id=1, source_target_pairs={{0,16},{4,20},{8,24},{12,28},{16,0},{20,4},{24,8},{28,12},{1,17},{... | collective-permute-start | bytes 1179656 | tf_op jit(solution)/shard_map/ppermute | solution.py:40
  68.7 3.5 %collective-permute-done.2 = f32[192,512]{1,0:T(8,128)} collective-permute-done((f32[192,512]{1,0:T(8,128)}, f32[192,512]{1,0:T(8,128)}, u32[]{:S(2)}, u32[]{:S(2)}) %collective-permute-start.2) | collective-permute-done | bytes 393248 | tf_op jit(solution)/shard_map/ppermute | solution.py:13
  72.2 1.0 bitcast_dynamic-update-slice_fusion.1
  73.2 0.8 slice_bitcast_fusion.4
  74.0 1.4 copy-done.5
  75.4 9.2 %collective-permute-done.8 = f32[192,512]{1,0:T(8,128)} collective-permute-done((f32[192,512]{1,0:T(8,128)}, f32[192,512]{1,0:T(8,128)}, u32[]{:S(2)}, u32[]{:S(2)}) %collective-permute-start.8) | collective-permute-done | bytes 393248 | tf_op jit(solution)/shard_map/ppermute | solution.py:40
  84.6 3.1 %convolution_bitcast_fusion.3 = f32[192,512]{1,0:T(8,128)} fusion(f32[192,384]{1,0:T(8,128)} %param.9, f32[192,512]{1,0:T(8,128)} %collective-permute-done.8, f32[192,512]{1,0:T(8,128)} %maximum_select_fusion.2, pred[]{:T(512)S(6)} %eq.9), kind=kOutput, calls=%fused_computation.19 | convolution fusion | flops 453574656 | bytes 1474561 | tf_op jit(solution)/shard_map/dot_general | solution.py:90
  87.7 1.8 %bitcast_dynamic-update-slice_fusion = f32[6,192,512]{2,1,0:T(8,128)} fusion(f32[6,192,512]{2,1,0:T(8,128)} %copy-done.5, f32[192,512]{1,0:T(8,128)} %collective-permute-done.3), kind=kLoop, calls=%fused_computation.60 | loop fusion | bytes 786432
  89.5 2.2 %slice_dynamic-update-slice_fusion = f32[6,192,512]{2,1,0:T(8,128)} fusion(f32[6,192,512]{2,1,0:T(8,128)} %bitcast_dynamic-update-slice_fusion, f32[3,192,512]{2,1,0:T(8,128)} %copy-done.1), kind=kLoop, calls=%fused_computation.30 | loop fusion | bytes 1572864
  91.6 1.8 %slice_dynamic-update-slice_fusion.1 = f32[6,192,512]{2,1,0:T(8,128)} fusion(f32[6,192,512]{2,1,0:T(8,128)} %slice_dynamic-update-slice_fusion, f32[3,192,512]{2,1,0:T(8,128)} %copy-done.1), kind=kLoop, calls=%fused_computation.53 | loop fusion | bytes 786432 | tf_op jit(solution)/shard_map/stack | solution.py:75
  93.4 4.0 %convolution_convert_fusion = bf16[6,512,192]{1,2,0:T(8,128)(2,1)S(1)} fusion(f32[6,192,512]{2,1,0:T(8,128)} %slice_dynamic-update-slice_fusion.1, f32[1,1,6,192,192]{4,3,2,1,0:T(8,128)S(1)} %copy-done.3), kind=kOutput, calls=%fused_computation.3 | convolution fusion | flops 1359544320 | bytes 4423680 | tf_op jit(solution)/shard_map/fij,fjr->fir/dot_general | solution.py:28
  97.4 3.4 %convolution_bitcast_fusion = f32[1152,512]{0,1:T(8,128)} fusion(bf16[1152,512]{1,0:T(8,128)(2,1)S(1)} %bitcast.126, bf16[1,1,1152,1152]{3,2,1,0:T(8,128)(2,1)S(1)} %copy-done), kind=kOutput, calls=%fused_computation | convolution fusion | flops 1358954496 | bytes 6193152 | tf_op jit(solution)/shard_map/dot_general | solution.py:101
  100.8 3.1 %copy.8 = f32[1152,512]{1,0:T(8,128)} copy(f32[1152,512]{0,1:T(8,128)} %convolution_bitcast_fusion) | data formatting | bytes 4718592 | tf_op jit(solution)/shard_map/dot_general | solution.py:101
  103.8 4.3 %convolution_bitcast_fusion.1 = f32[6,192,512]{2,1,0:T(8,128)S(1)} fusion(f32[6,192,512]{2,1,0:T(8,128)} %bitcast.125, f32[1,1,6,192,192]{4,3,2,1,0:T(8,128)} %param.6), kind=kOutput, calls=%fused_computation.2 | convolution fusion | flops 1358954496 | bytes 5603328 | tf_op jit(solution)/shard_map/fij,fjr->fir/dot_general | solution.py:28
  108.2 1.1 slice_bitcast_fusion.2
  110.0 11.9 %collective-permute-start.4 = (f32[192,512]{1,0:T(8,128)}, f32[192,512]{1,0:T(8,128)}, u32[]{:S(2)}, u32[]{:S(2)}) collective-permute-start(f32[192,512]{1,0:T(8,128)} %get-tuple-element.7), channel_id=1, source_target_pairs={{0,28},{4,0},{8,4},{12,8},{16,12},{20,16},{24,20},{28,24},{1,29},{... | collective-permute-start | bytes 1179656 | tf_op jit(solution)/shard_map/ppermute | solution.py:13
  121.9 2.8 %collective-permute-start.5 = (f32[192,512]{1,0:T(8,128)}, f32[192,512]{1,0:T(8,128)}, u32[]{:S(2)}, u32[]{:S(2)}) collective-permute-start(f32[192,512]{1,0:T(8,128)} %get-tuple-element.9), channel_id=1, source_target_pairs={{0,3},{1,0},{2,1},{3,2},{4,7},{5,4},{6,5},{7,6},{8,11},{9,8},{10,9... | collective-permute-start | bytes 1179656 | tf_op jit(solution)/shard_map/ppermute | solution.py:13
  124.7 6.6 %all-reduce.2.cloned.1.call-done = f32[192,512]{1,0:T(8,128)} async-done(((f32[192,512]{1,0:T(8,128)}), f32[192,512]{1,0:T(8,128)}) %all-reduce.2.cloned.1.call-update) | async-done | bytes 393232 | tf_op jit(solution)/shard_map/psum | solution.py:97
  131.2 0.9 constant_dynamic-slice_fusion
  132.1 1.1 convolution_bitcast_fusion.2
  133.3 1.5 %fusion.22 = (f32[1,192,512]{2,1,0:T(8,128)S(1)}, f32[1,192,512]{2,1,0:T(8,128)S(1)}) fusion(f32[192,512]{1,0:T(8,128)} %collective-permute-done.4, f32[6,192,512]{2,1,0:T(8,128)} %copy-done.4, f32[192,512]{1,0:T(8,128)} %collective-permute-done.5), kind=kLoop, calls=%fused_computation.52 | loop fusion | flops 196608 | bytes 2359296 | tf_op jit(solution)/shard_map/stack | solution.py:106
  134.8 2.2 %fusion.1 = f32[1,1,3,192,512]{4,3,2,1,0:T(8,128)} fusion(f32[3,192,512]{2,1,0:T(8,128)S(1)} %convolution_bitcast_fusion.2, f32[3,192,192]{2,1,0:T(8,128)S(1)} %convolution_subtract_fusion, f32[1,192,512]{2,1,0:T(8,128)S(1)} %copy-done.7, f32[1,192,512]{2,1,0:T(8,128)S(1)} %get-tuple-element.6, f32[1,192,512]{2,1,0:T(8,128)S(1)} %get-tuple-element.5), kind=kOutput, calls=%fused_computation.6 | convolution fusion | flops 680361984 | bytes 3981312 | tf_op jit(solution)/shard_map/fij,fjr->fir/dot_general | solution.py:28
  (46 shorter events, 12.9 us)
Async XLA Ops:
  6.5 90.8 %copy-start = (bf16[1,1,1152,1152]{3,2,1,0:T(8,128)(2,1)S(1)}, bf16[1,1,1152,1152]{3,2,1,0:T(8,128)(2,1)}, u32[]{:S(2)}) copy-start(bf16[1,1,1152,1152]{3,2,1,0:T(8,128)(2,1)} %param.7) | copy-start | bytes 7962628
  6.5 124.7 %all-reduce.2.cloned.1.call-start = ((), (), s32[]{:S(2)}) async-start(), calls=%async_computation | async-start | bytes 786432 | tf_op jit(solution)/shard_map/psum | solution.py:97
  11.2 10.1 %collective-permute-start.1 = (f32[192,704]{1,0:T(8,128)}, f32[192,704]{1,0:T(8,128)S(1)}, u32[]{:S(2)}, u32[]{:S(2)}) collective-permute-start(f32[192,704]{1,0:T(8,128)} %pad_maximum_fusion.4), channel_id=1, source_target_pairs={{0,3},{1,0},{2,1},{3,2},{4,7},{5,4},{6,5},{7,6},{8,11},{9,8},{10,9... | collective-permute-start | bytes 1622024 | tf_op jit(solution)/shard_map/ppermute | solution.py:13
  14.7 17.2 %collective-permute-start = (f32[192,704]{1,0:T(8,128)}, f32[192,704]{1,0:T(8,128)}, u32[]{:S(2)}, u32[]{:S(2)}) collective-permute-start(f32[192,704]{1,0:T(8,128)} %pad_maximum_fusion.3), channel_id=1, source_target_pairs={{0,28},{4,0},{8,4},{12,8},{16,12},{20,16},{24,20},{28,24},{1,29},{... | collective-permute-start | bytes 1622024 | tf_op jit(solution)/shard_map/ppermute | solution.py:13
  21.4 0.8 copy-start.8
  33.4 1.8 %copy-start.6 = (f32[1,192,512]{2,1,0:T(8,128)S(1)}, f32[1,192,512]{2,1,0:T(8,128)}, u32[]{:S(2)}) copy-start(f32[1,192,512]{2,1,0:T(8,128)} %get-tuple-element.14) | copy-start | bytes 1179652
  33.5 1.8 %copy-start.9 = (f32[3,192,16]{1,2,0:T(8,128)S(1)}, f32[3,192,16]{1,2,0:T(8,128)}, u32[]{:S(2)}) copy-start(f32[3,192,16]{1,2,0:T(8,128)} %param.8) | copy-start | bytes 110596
  36.0 22.8 %collective-permute-start.6 = (f32[48,512]{1,0:T(8,128)S(1)}, f32[48,512]{1,0:T(8,128)S(1)}, u32[]{:S(2)}, u32[]{:S(2)}) collective-permute-start(f32[48,512]{1,0:T(8,128)S(1)} %bitcast.128), channel_id=1, source_target_pairs={{0,4},{4,0},{8,12},{12,8},{16,20},{20,16},{24,28},{28,24},{1,5},{5... | collective-permute-start | bytes 294920 | tf_op jit(solution)/shard_map/ppermute | solution.py:40
  55.2 1.0 copy-start.1
  57.0 15.1 %collective-permute-start.2 = (f32[192,512]{1,0:T(8,128)}, f32[192,512]{1,0:T(8,128)}, u32[]{:S(2)}, u32[]{:S(2)}) collective-permute-start(f32[192,512]{1,0:T(8,128)} %slice_bitcast_fusion.7), channel_id=1, source_target_pairs={{0,4},{4,8},{8,12},{12,16},{16,20},{20,24},{24,28},{28,0},{1,5},{5... | collective-permute-start | bytes 1179656 | tf_op jit(solution)/shard_map/ppermute | solution.py:13
  58.7 5.8 %collective-permute-start.7 = (f32[96,512]{1,0:T(8,128)S(1)}, f32[96,512]{1,0:T(8,128)}, u32[]{:S(2)}, u32[]{:S(2)}) collective-permute-start(f32[96,512]{1,0:T(8,128)S(1)} %maximum_select_fusion.3), channel_id=1, source_target_pairs={{0,8},{4,12},{8,0},{12,4},{16,24},{20,28},{24,16},{28,20},{1,9},{5... | collective-permute-start | bytes 589832 | tf_op jit(solution)/shard_map/ppermute | solution.py:40
  58.8 14.4 %copy-start.2 = (f32[3,192,512]{2,1,0:T(8,128)S(1)}, f32[3,192,512]{2,1,0:T(8,128)}, u32[]{:S(2)}) copy-start(f32[3,192,512]{2,1,0:T(8,128)} %copy-done.1) | copy-start | bytes 3538948
  66.4 18.2 %collective-permute-start.8 = (f32[192,512]{1,0:T(8,128)}, f32[192,512]{1,0:T(8,128)}, u32[]{:S(2)}, u32[]{:S(2)}) collective-permute-start(f32[192,512]{1,0:T(8,128)} %maximum_select_fusion.2), channel_id=1, source_target_pairs={{0,16},{4,20},{8,24},{12,28},{16,0},{20,4},{24,8},{28,12},{1,17},{... | collective-permute-start | bytes 1179656 | tf_op jit(solution)/shard_map/ppermute | solution.py:40
  74.0 1.4 copy-start.5
  75.4 12.2 %collective-permute-start.3 = (f32[192,512]{1,0:T(8,128)}, f32[192,512]{1,0:T(8,128)}, u32[]{:S(2)}, u32[]{:S(2)}) collective-permute-start(f32[192,512]{1,0:T(8,128)} %get-tuple-element.15), channel_id=1, source_target_pairs={{0,1},{1,2},{2,3},{3,0},{4,5},{5,6},{6,7},{7,4},{8,9},{9,10},{10,1... | collective-permute-start | bytes 1179656 | tf_op jit(solution)/shard_map/ppermute | solution.py:13
  89.4 3.9 %copy-start.3 = (f32[1,1,6,192,192]{4,3,2,1,0:T(8,128)S(1)}, f32[1,1,6,192,192]{4,3,2,1,0:T(8,128)}, u32[]{:S(2)}) copy-start(f32[1,1,6,192,192]{4,3,2,1,0:T(8,128)} %param.6) | copy-start | bytes 2654212
  108.2 1.8 %copy-start.4 = (f32[6,192,512]{2,1,0:T(8,128)}, f32[6,192,512]{2,1,0:T(8,128)S(1)}, u32[]{:S(2)}) copy-start(f32[6,192,512]{2,1,0:T(8,128)S(1)} %convolution_bitcast_fusion.1) | copy-start | bytes 7077892
  110.0 23.3 %collective-permute-start.4 = (f32[192,512]{1,0:T(8,128)}, f32[192,512]{1,0:T(8,128)}, u32[]{:S(2)}, u32[]{:S(2)}) collective-permute-start(f32[192,512]{1,0:T(8,128)} %get-tuple-element.7), channel_id=1, source_target_pairs={{0,28},{4,0},{8,4},{12,8},{16,12},{20,16},{24,20},{28,24},{1,29},{... | collective-permute-start | bytes 1179656 | tf_op jit(solution)/shard_map/ppermute | solution.py:13
  121.9 11.4 %collective-permute-start.5 = (f32[192,512]{1,0:T(8,128)}, f32[192,512]{1,0:T(8,128)}, u32[]{:S(2)}, u32[]{:S(2)}) collective-permute-start(f32[192,512]{1,0:T(8,128)} %get-tuple-element.9), channel_id=1, source_target_pairs={{0,3},{1,0},{2,1},{3,2},{4,7},{5,4},{6,5},{7,6},{8,11},{9,8},{10,9... | collective-permute-start | bytes 1179656 | tf_op jit(solution)/shard_map/ppermute | solution.py:13
  133.3 1.6 %copy-start.7 = (f32[1,192,512]{2,1,0:T(8,128)S(1)}, f32[1,192,512]{2,1,0:T(8,128)}, u32[]{:S(2)}) copy-start(f32[1,192,512]{2,1,0:T(8,128)} %get-tuple-element.8) | copy-start | bytes 1179652
Sparse Core Ops, SparseCore 0:
  87.8 43.4 all-reduce.1
